TPU v7x, 512 devices: a whole 4x8x8 slice. The times are simulated.
512 devices in a mesh: grp: 8 (over y_lo, x), sub: 64 (over z, y_hi, core).
Axes of the slice: x: 4, y: 8 (y_hi: 4, y_lo: 2; y = y_hi * 2 + y_lo), z: 8, core: 2. Of those that a mesh axis runs over, the one named last changes fastest.
Arguments:
- schur_t: bfloat16 [8, 64, 1024, 1024], P('grp', 'sub')
- neumann_t: bfloat16 [8, 64, 1024, 1024], P('grp', 'sub')
- face_weights: float32 [8, 64, 1024], P('grp', 'sub'), as said below
- coarse_basis: bfloat16 [8, 64, 1024, 24], P('grp', 'sub'), may hold values from -0.375 to 0.375
- coarse_inverse: float32 [8, 768, 768], P('grp', 'sub')
- coarse_number: int32 [8, 1536], P('grp'), may hold values from 0 to 767, as said below
- loads: bfloat16 [8, 64, 1024, 128], P('grp', 'sub'), may hold values from -6 to 6
- iterate: bfloat16 [8, 64, 1024, 128], P('grp', 'sub'), as said below
Outputs:
- iterate_out: bfloat16 [8, 64, 1024, 128], P('grp', 'sub')
Inputs may be any that keep to these rules, and one draw needn't show every extreme that they name: `face_weights`: the weights of an unknown and of its partner unknown on the face it shares sum to one. `coarse_number`: each value appears exactly twice in each group's row. `iterate`: equal on the two copies of each shared unknown.
All inputs are finite; a program needn't handle non-finite values.
Results may differ from a plain program's by a relative error of at most 0.0051.
Values sent between devices are 32-bit elements; how exact they have to be, the bound alone decides.
A program may use at most 64 MiB of HBM per device.

v0:
```python
import jax
import jax.numpy as jnp
from jax import lax
from jax.sharding import PartitionSpec as P

ITERS = 3


def extended(array, sides, width):
    for axis, dim in sides:
        devices, length = (lax.axis_size(axis), array.shape[dim])
        up = [(i, (i + 1) % devices) for i in range(devices)]
        down = [(j, i) for i, j in up]
        last = lax.slice_in_dim(array, length - width, length, axis=dim)
        leading = lax.slice_in_dim(array, 0, width, axis=dim)
        before = lax.ppermute(last, axis, up)
        after = lax.ppermute(leading, axis, down)
        array = jnp.concatenate([before, array, after], axis=dim)
    return array


def add_partners(local):
    face = local.shape[0] // 4
    columns = local.shape[1]
    faces = local.reshape(4, face, columns)
    along_sub = extended(faces[0:2], (("sub", 0),), 1)
    along_grp = extended(faces[2:4], (("grp", 0),), 1)
    summed = jnp.stack(
        [
            faces[0] + along_sub[0],
            faces[1] + along_sub[3],
            faces[2] + along_grp[0],
            faces[3] + along_grp[3],
        ]
    )
    return summed.reshape(4 * face, columns)


def shards(
    schur_t, neumann_t, face_weights, coarse_basis, coarse_inverse, coarse_number, loads, iterate
):
    schur = schur_t[0, 0]
    neumann = neumann_t[0, 0]
    weights = face_weights[0, 0][:, None]
    basis = coarse_basis[0, 0]
    basis_wide = basis.astype(jnp.float32)
    basis_across = basis.T
    inverse_rows = coarse_inverse[0]
    numbers = coarse_number[0]
    per_sub = basis.shape[1]
    coarse_order = inverse_rows.shape[1]
    highest = lax.Precision.HIGHEST
    own = lax.dynamic_slice_in_dim(numbers, lax.axis_index("sub") * per_sub, per_sub)
    load_wide = loads[0, 0].astype(jnp.float32)
    current = iterate[0, 0]
    for step in range(ITERS):
        image = jnp.dot(schur, current, preferred_element_type=jnp.float32)
        resid = add_partners(load_wide - image)
        weighted = (weights * resid).astype(jnp.bfloat16)
        local_coarse = jnp.dot(basis_across, weighted, preferred_element_type=jnp.float32)
        scattered = jax.ops.segment_sum(local_coarse, own, num_segments=coarse_order)
        coarse_rhs = lax.psum(scattered, "sub")
        solved_rows = jnp.dot(inverse_rows, coarse_rhs, precision=highest)
        solved = lax.all_gather(solved_rows, "sub", axis=0, tiled=True)
        own_values = jnp.take(solved, own, axis=0)
        fine = jnp.dot(neumann, weighted, preferred_element_type=jnp.float32)
        correction = fine + jnp.dot(basis_wide, own_values, precision=highest)
        update = add_partners(weights * correction)
        current = (current.astype(jnp.float32) + update).astype(jnp.bfloat16)
    return current[None, None]


def solution(mesh):
    return jax.shard_map(
        shards,
        mesh=mesh,
        in_specs=(
            P("grp", "sub", None, None),
            P("grp", "sub", None, None),
            P("grp", "sub", None),
            P("grp", "sub", None, None),
            P("grp", "sub", None),
            P("grp", None),
            P("grp", "sub", None, None),
            P("grp", "sub", None, None),
        ),
        out_specs=P("grp", "sub", None, None),
        check_vma=False,
    )
```

profile of v0, /device:TPU:241, one launch (start us, length us, event | category | flops | bytes accessed | tf_op | source)
XLA Modules:
  0.0 2029.4 jit_solution(9209375182098139773)
XLA Ops:
  10.6 5.1 collective-permute-start
  15.6 3.1 collective-permute-start.2
  18.8 4.3 collective-permute-start.3
  27.5 7.6 collective-permute-done.1
  38.0 3.2 fusion.4
  41.2 531.6 %all-reduce.4.cloned.1.call-done = f32[768,128]{1,0:T(8,128)} async-done(((f32[768,128]{1,0:T(8,128)}), f32[768,128]{1,0:T(8,128)}) %all-reduce.4.cloned.1.call-update) | async-done | bytes 393232 | tf_op jit(solution)/shard_map/psum | solution.py:62
  574.1 76.8 %all-gather = f32[64,12,128]{2,1,0:T(8,128)S(1)} all-gather(f32[1,12,128]{2,1,0:T(8,128)S(1)} %convolution_bitcast_fusion.5), channel_id=1, replica_groups=mesh['grp'=8,'sub'=64] {'sub'}, dimensions={0}, use_global_device_ids=true | all-gather | bytes 399360 | tf_op jit(solution)/shard_map/all_gather | solution.py:64
  653.9 7.6 collective-permute-start.4
  661.5 3.1 collective-permute-start.6
  664.6 4.3 collective-permute-start.7
  672.5 8.6 collective-permute-done.5
  689.0 5.5 collective-permute-start.11
  694.5 3.0 collective-permute-start.9
  697.5 7.7 collective-permute-done.9
  707.1 3.2 fusion.2
  710.3 531.1 %all-reduce.6.cloned.1.call-done = f32[768,128]{1,0:T(8,128)} async-done(((f32[768,128]{1,0:T(8,128)}), f32[768,128]{1,0:T(8,128)}) %all-reduce.6.cloned.1.call-update) | async-done | bytes 393232 | tf_op jit(solution)/shard_map/psum | solution.py:62
  1242.8 76.8 %all-gather.1 = f32[64,12,128]{2,1,0:T(8,128)S(1)} all-gather(f32[1,12,128]{2,1,0:T(8,128)S(1)} %convolution_bitcast_fusion.4), channel_id=1, replica_groups=mesh['grp'=8,'sub'=64] {'sub'}, dimensions={0}, use_global_device_ids=true | all-gather | bytes 399360 | tf_op jit(solution)/shard_map/all_gather | solution.py:64
  1323.6 7.6 collective-permute-start.12
  1331.2 3.1 collective-permute-start.14
  1334.3 4.3 collective-permute-start.15
  1340.5 9.9 collective-permute-done.13
  1356.2 5.5 collective-permute-start.19
  1361.7 3.0 collective-permute-start.17
  1364.7 7.7 collective-permute-done.17
  1374.2 3.2 fusion
  1377.5 531.1 %all-reduce.8.cloned.1.call-done = f32[768,128]{1,0:T(8,128)} async-done(((f32[768,128]{1,0:T(8,128)}), f32[768,128]{1,0:T(8,128)}) %all-reduce.8.cloned.1.call-update) | async-done | bytes 393232 | tf_op jit(solution)/shard_map/psum | solution.py:62
  1909.9 76.8 %all-gather.2 = f32[64,12,128]{2,1,0:T(8,128)S(1)} all-gather(f32[1,12,128]{2,1,0:T(8,128)S(1)} %convolution_bitcast_fusion.3), channel_id=1, replica_groups=mesh['grp'=8,'sub'=64] {'sub'}, dimensions={0}, use_global_device_ids=true | all-gather | bytes 399360 | tf_op jit(solution)/shard_map/all_gather | solution.py:64
  1991.4 7.6 collective-permute-start.20
  1999.1 3.1 collective-permute-start.22
  2002.2 4.3 collective-permute-start.23
  2009.4 2.0 copy.23
  2011.5 7.2 collective-permute-done.21
  (105 shorter events, 56.6 us)
Async XLA Ops:
  6.5 18.9 copy-start.10
  6.5 566.2 %all-reduce.4.cloned.1.call-start = ((), (), s32[]{:S(2)}) async-start(), calls=%async_computation | async-start | bytes 786432 | tf_op jit(solution)/shard_map/psum | solution.py:62
  9.9 26.5 %copy-start.5 = (bf16[1,1,1024,24]{2,3,1,0:T(8,128)(2,1)S(1)}, bf16[1,1,1024,24]{2,3,1,0:T(8,128)(2,1)}, u32[]{:S(2)}) copy-start(bf16[1,1,1024,24]{2,3,1,0:T(8,128)(2,1)} %param.13) | copy-start | bytes 147460
  10.6 16.3 collective-permute-start
  15.6 11.2 collective-permute-start.2
  18.8 8.1 collective-permute-start.3
  23.1 12.0 collective-permute-start.1
  36.3 536.5 %copy-start.6 = (f32[1,12,768]{2,0,1:T(1,128)S(1)}, f32[1,12,768]{2,0,1:T(1,128)}, u32[]{:S(2)}) copy-start(f32[1,12,768]{2,0,1:T(1,128)} %param.14) | copy-start | bytes 110596
  37.9 1203.5 %all-reduce.6.cloned.1.call-start = ((), (), s32[]{:S(2)}) async-start(), calls=%async_computation.1 | async-start | bytes 786432 | tf_op jit(solution)/shard_map/psum | solution.py:62
  41.2 629.7 %copy-start.2 = (bf16[1,1,1024,128]{3,2,1,0:T(8,128)(2,1)S(1)}, bf16[1,1,1024,128]{3,2,1,0:T(8,128)(2,1)}, u32[]{:S(2)}) copy-start(bf16[1,1,1024,128]{3,2,1,0:T(8,128)(2,1)} %param.17) | copy-start | bytes 786436
  653.9 17.9 collective-permute-start.4
  661.5 10.3 collective-permute-start.6
  664.6 7.2 collective-permute-start.7
  668.9 12.2 collective-permute-start.5
  685.1 12.3 collective-permute-start.8
  687.1 10.4 collective-permute-start.10
  689.0 8.5 collective-permute-start.11
  694.5 10.7 collective-permute-start.9
  707.1 1201.5 %all-reduce.8.cloned.1.call-start = ((), (), s32[]{:S(2)}) async-start(), calls=%async_computation.2 | async-start | bytes 786432 | tf_op jit(solution)/shard_map/psum | solution.py:62
  1323.6 17.0 collective-permute-start.12
  1331.2 9.3 collective-permute-start.14
  1334.3 6.3 collective-permute-start.15
  1338.6 11.9 collective-permute-start.13
  1352.4 12.3 collective-permute-start.16
  1354.3 10.4 collective-permute-start.18
  1356.2 8.5 collective-permute-start.19
  1361.7 10.7 collective-permute-start.17
  1377.5 630.9 %copy-start.3 = (f32[4,256,128]{1,2,0:T(8,128)S(1)}, f32[4,256,128]{1,2,0:T(8,128)}, u32[]{:S(2)}) copy-start(f32[4,256,128]{1,2,0:T(8,128)} %get-tuple-element.8) | copy-start | bytes 1572868
  1991.4 20.0 collective-permute-start.20
  1999.1 12.4 collective-permute-start.22
  2002.2 9.3 collective-permute-start.23
  2006.5 12.2 collective-permute-start.21
  (6 other events, 25.6 us)
Sparse Core Ops, SparseCore 0:
  38.0 534.7 all-reduce.3
  707.2 534.2 all-reduce.5
  1374.4 534.2 all-reduce.7
where the time goes:
time: 2030 us
  waiting for transfers between devices  1640 us (81%)
  blocking collectives  231 us (11%)
  starting transfers between devices  89.8 us (4%)
  matrix products  21.8 us (1%)
    psum x3, waiting for transfers between devices, shards(): coarse_rhs = lax.psum(scattered, 'sub')  1590 us
    all_gather x3, blocking collectives, shards(): solved = lax.all_gather(solved_rows, 'sub', axis=0, tiled=True)  231 us
    ppermute x12, waiting for transfers between devices, extended(): after = lax.ppermute(leading, axis, down)  48.7 us
    ppermute x12, starting transfers between devices, extended(): before = lax.ppermute(last, axis, up)  48 us
    ppermute x12, starting transfers between devices, extended(): after = lax.ppermute(leading, axis, down)  41.7 us
  transfers between devices with their start and end apart: 27, of which 9 were waited for; matrix products, arithmetic and copies ran while one was open for 1% of the time, Pallas kernels for 0%

commit v1 on v0

--- a/solution.py
+++ b/solution.py
@@ -59,7 +59,7 @@
         weighted = (weights * resid).astype(jnp.bfloat16)
         local_coarse = jnp.dot(basis_across, weighted, preferred_element_type=jnp.float32)
         scattered = jax.ops.segment_sum(local_coarse, own, num_segments=coarse_order)
-        coarse_rhs = lax.psum(scattered, "sub")
+        coarse_rhs = jnp.sum(lax.all_gather(scattered, "sub"), axis=0)
         solved_rows = jnp.dot(inverse_rows, coarse_rhs, precision=highest)
         solved = lax.all_gather(solved_rows, "sub", axis=0, tiled=True)
         own_values = jnp.take(solved, own, axis=0)

time: 2030 us -> 988 us (0.49)
  the two profiles are of different devices: /device:TPU:241 before, /device:TPU:14 now
where the time goes in v1:
time: 988 us; the launch traced here: 986 us
  waiting for transfers between devices  538 us (54%)
  blocking collectives  253 us (26%)
  starting transfers between devices  99.9 us (10%)
  other arithmetic  42.3 us (4%)
  matrix products  19.9 us (2%)
  local copies, waits for them, and re-layouts  19.5 us (2%)
  between operations  13.6 us (1%)
    all_gather x3, waiting for transfers between devices, shards(): coarse_rhs = jnp.sum(lax.all_gather(scattered, 'sub'), axis=0)  510 us
    all_gather x3, blocking collectives, shards(): solved = lax.all_gather(solved_rows, 'sub', axis=0, tiled=True)  253 us
    ppermute x12, starting transfers between devices, extended(): after = lax.ppermute(leading, axis, down)  67.8 us
    ppermute x12, starting transfers between devices, extended(): before = lax.ppermute(last, axis, up)  32.1 us
    reduce_sum x3, other arithmetic, shards(): coarse_rhs = jnp.sum(lax.all_gather(scattered, 'sub'), axis=0)  27.9 us
    ppermute x12, waiting for transfers between devices, extended(): after = lax.ppermute(leading, axis, down)  24.5 us
  transfers between devices with their start and end apart: 27, of which 13 were waited for; matrix products, arithmetic and copies ran while one was open for 2% of the time, Pallas kernels for 0%

profile of v1, /device:TPU:14, one launch (start us, length us, event | category | flops | bytes accessed | tf_op | source)
XLA Modules:
  0.0 986.0 jit_solution(6942206534197960391)
XLA Ops:
  12.5 13.2 %collective-permute-start.1 = (f32[1,256,128]{2,1,0:T(8,128)S(1)}, f32[1,256,128]{2,1,0:T(8,128)S(1)}, u32[]{:S(2)}, u32[]{:S(2)}) collective-permute-start(f32[1,256,128]{2,1,0:T(8,128)S(1)} %get-tuple-element.59), channel_id=1, source_target_pairs={{1,0},{2,1},{3,2},{4,3},{5,4},{6,5},{7,6},{8,7},{9,8},{10,9},{11,1... | collective-permute-start | bytes 393224 | tf_op jit(solution)/shard_map/ppermute | solution.py:17
  25.7 3.2 collective-permute-start.2
  28.9 2.7 collective-permute-start.3
  34.1 3.8 collective-permute-done.3
  40.8 3.3 fusion.4
  44.1 169.8 %all-gather.10.cloned.1.call-done = f32[49152,128]{1,0:T(8,128)} async-done(((f32[768,128]{1,0:T(8,128)}), f32[49152,128]{1,0:T(8,128)}) %all-gather.10.cloned.1.call-update) | async-done | bytes 25165840 | tf_op jit(solution)/shard_map/all_gather | solution.py:62
  213.9 9.0 reduce_sum.27
  223.3 82.5 %all-gather.3 = f32[64,12,128]{2,1,0:T(8,128)S(1)} all-gather(f32[1,12,128]{2,1,0:T(8,128)S(1)} %convolution_bitcast_fusion.5), channel_id=1, replica_groups=mesh['grp'=8,'sub'=64] {'sub'}, dimensions={0}, use_global_device_ids=true | all-gather | bytes 399360 | tf_op jit(solution)/shard_map/all_gather | solution.py:64
  312.7 7.5 collective-permute-start.5
  320.2 4.2 collective-permute-start.6
  327.4 6.3 collective-permute-done.7
  339.5 3.9 collective-permute-start.11
  345.4 7.9 collective-permute-start.9
  357.7 3.3 fusion.2
  361.0 171.5 %all-gather.12.cloned.1.call-done = f32[49152,128]{1,0:T(8,128)} async-done(((f32[768,128]{1,0:T(8,128)}), f32[49152,128]{1,0:T(8,128)}) %all-gather.12.cloned.1.call-update) | async-done | bytes 25165840 | tf_op jit(solution)/shard_map/all_gather | solution.py:62
  532.4 9.8 reduce_sum.28
  543.5 87.7 %all-gather.4 = f32[64,12,128]{2,1,0:T(8,128)} all-gather(f32[1,12,128]{2,1,0:T(8,128)S(1)} %convolution_bitcast_fusion.4), channel_id=1, replica_groups=mesh['grp'=8,'sub'=64] {'sub'}, dimensions={0}, use_global_device_ids=true | all-gather | bytes 399360 | tf_op jit(solution)/shard_map/all_gather | solution.py:64
  636.2 2.3 collective-permute-start.12
  638.5 7.5 collective-permute-start.13
  646.0 4.2 collective-permute-start.14
  652.9 6.3 collective-permute-done.15
  663.0 7.9 collective-permute-start.17
  672.8 3.9 collective-permute-start.19
  677.8 4.0 collective-permute-done.19
  683.7 3.2 fusion
  686.9 168.9 %all-gather.14.cloned.1.call-done = f32[49152,128]{1,0:T(8,128)} async-done(((f32[768,128]{1,0:T(8,128)}), f32[49152,128]{1,0:T(8,128)}) %all-gather.14.cloned.1.call-update) | async-done | bytes 25165840 | tf_op jit(solution)/shard_map/all_gather | solution.py:62
  855.8 9.0 reduce_sum.29
  865.1 82.5 %all-gather.5 = f32[64,12,128]{2,1,0:T(8,128)S(1)} all-gather(f32[1,12,128]{2,1,0:T(8,128)S(1)} %convolution_bitcast_fusion.3), channel_id=1, replica_groups=mesh['grp'=8,'sub'=64] {'sub'}, dimensions={0}, use_global_device_ids=true | all-gather | bytes 399360 | tf_op jit(solution)/shard_map/all_gather | solution.py:64
  952.3 2.2 collective-permute-start.20
  954.5 7.5 collective-permute-start.21
  962.0 4.2 collective-permute-start.22
  972.3 3.1 collective-permute-done.23
  (100 shorter events, 66.2 us)
Async XLA Ops:
  6.5 25.5 %copy-start.6 = (f32[1,1,1024]{2,1,0:T(1,128)S(1)}, f32[1,1,1024]{2,1,0:T(1,128)}, u32[]{:S(2)}) copy-start(f32[1,1,1024]{2,1,0:T(1,128)} %param.12) | copy-start | bytes 12292
  6.5 207.3 %all-gather.10.cloned.1.call-start = ((), (), s32[]{:S(2)}) async-start(), calls=%async_computation | async-start | bytes 25559040 | tf_op jit(solution)/shard_map/all_gather | solution.py:62
  9.9 29.3 %copy-start.3 = (bf16[1,1,1024,24]{2,3,1,0:T(8,128)(2,1)S(1)}, bf16[1,1,1024,24]{2,3,1,0:T(8,128)(2,1)}, u32[]{:S(2)}) copy-start(bf16[1,1,1024,24]{2,3,1,0:T(8,128)(2,1)} %param.13) | copy-start | bytes 147460
  10.6 22.9 %collective-permute-start = (f32[1,256,128]{2,1,0:T(8,128)}, f32[1,256,128]{2,1,0:T(8,128)S(1)}, u32[]{:S(2)}, u32[]{:S(2)}) collective-permute-start(f32[1,256,128]{2,1,0:T(8,128)} %get-tuple-element.56), channel_id=1, source_target_pairs={{0,1},{1,2},{2,3},{3,4},{4,5},{5,6},{6,7},{7,8},{8,9},{9,10},{10,1... | collective-permute-start | bytes 393224 | tf_op jit(solution)/shard_map/ppermute | solution.py:16
  12.5 21.0 %collective-permute-start.1 = (f32[1,256,128]{2,1,0:T(8,128)S(1)}, f32[1,256,128]{2,1,0:T(8,128)S(1)}, u32[]{:S(2)}, u32[]{:S(2)}) collective-permute-start(f32[1,256,128]{2,1,0:T(8,128)S(1)} %get-tuple-element.59), channel_id=1, source_target_pairs={{1,0},{2,1},{3,2},{4,3},{5,4},{6,5},{7,6},{8,7},{9,8},{10,9},{11,1... | collective-permute-start | bytes 393224 | tf_op jit(solution)/shard_map/ppermute | solution.py:17
  25.7 7.8 collective-permute-start.2
  28.9 9.1 collective-permute-start.3
  40.8 491.7 %all-gather.12.cloned.1.call-start = ((), (), s32[]{:S(2)}) async-start(), calls=%async_computation.1 | async-start | bytes 25559040 | tf_op jit(solution)/shard_map/all_gather | solution.py:62
  213.9 9.0 copy-start.4
  222.9 103.4 %copy-start.2 = (bf16[1,1,1024,128]{3,2,1,0:T(8,128)(2,1)S(1)}, bf16[1,1,1024,128]{3,2,1,0:T(8,128)(2,1)}, u32[]{:S(2)}) copy-start(bf16[1,1,1024,128]{3,2,1,0:T(8,128)(2,1)} %param.17) | copy-start | bytes 786436
  310.4 16.9 %collective-permute-start.4 = (f32[1,256,128]{1,2,0:T(8,128)}, f32[1,256,128]{1,2,0:T(8,128)S(1)}, u32[]{:S(2)}, u32[]{:S(2)}) collective-permute-start(f32[1,256,128]{1,2,0:T(8,128)} %get-tuple-element.48), channel_id=1, source_target_pairs={{0,1},{1,2},{2,3},{3,4},{4,5},{5,6},{6,7},{7,8},{8,9},{9,10},{10,1... | collective-permute-start | bytes 393224 | tf_op jit(solution)/shard_map/ppermute | solution.py:16
  312.7 14.6 %collective-permute-start.5 = (f32[1,256,128]{1,2,0:T(8,128)}, f32[1,256,128]{1,2,0:T(8,128)S(1)}, u32[]{:S(2)}, u32[]{:S(2)}) collective-permute-start(f32[1,256,128]{1,2,0:T(8,128)} %get-tuple-element.51), channel_id=1, source_target_pairs={{1,0},{2,1},{3,2},{4,3},{5,4},{6,5},{7,6},{8,7},{9,8},{10,9},{11,1... | collective-permute-start | bytes 393224 | tf_op jit(solution)/shard_map/ppermute | solution.py:17
  320.2 7.2 collective-permute-start.6
  324.4 9.3 collective-permute-start.7
  327.3 9.5 copy-start.1
  337.6 15.7 %collective-permute-start.10 = (f32[1,256,128]{2,1,0:T(8,128)S(1)}, f32[1,256,128]{2,1,0:T(8,128)S(1)}, u32[]{:S(2)}, u32[]{:S(2)}) collective-permute-start(f32[1,256,128]{2,1,0:T(8,128)S(1)} %get-tuple-element.41), channel_id=1, source_target_pairs={{0,64},{64,128},{128,192},{192,256},{256,320},{320,384},{384,448},... | collective-permute-start | bytes 393224 | tf_op jit(solution)/shard_map/ppermute | solution.py:16
  339.5 13.7 %collective-permute-start.11 = (f32[1,256,128]{2,1,0:T(8,128)S(1)}, f32[1,256,128]{2,1,0:T(8,128)S(1)}, u32[]{:S(2)}, u32[]{:S(2)}) collective-permute-start(f32[1,256,128]{2,1,0:T(8,128)S(1)} %get-tuple-element.42), channel_id=1, source_target_pairs={{64,0},{128,64},{192,128},{256,192},{320,256},{384,320},{448,384},... | collective-permute-start | bytes 393224 | tf_op jit(solution)/shard_map/ppermute | solution.py:17
  343.5 11.4 %collective-permute-start.8 = (f32[1,256,128]{2,1,0:T(8,128)S(1)}, f32[1,256,128]{2,1,0:T(8,128)S(1)}, u32[]{:S(2)}, u32[]{:S(2)}) collective-permute-start(f32[1,256,128]{2,1,0:T(8,128)S(1)} %get-tuple-element.40), channel_id=1, source_target_pairs={{0,1},{1,2},{2,3},{3,4},{4,5},{5,6},{6,7},{7,8},{8,9},{9,10},{10,1... | collective-permute-start | bytes 393224 | tf_op jit(solution)/shard_map/ppermute | solution.py:16
  345.4 10.4 %collective-permute-start.9 = (f32[1,256,128]{2,1,0:T(8,128)S(1)}, f32[1,256,128]{2,1,0:T(8,128)S(1)}, u32[]{:S(2)}, u32[]{:S(2)}) collective-permute-start(f32[1,256,128]{2,1,0:T(8,128)S(1)} %get-tuple-element.43), channel_id=1, source_target_pairs={{1,0},{2,1},{3,2},{4,3},{5,4},{6,5},{7,6},{8,7},{9,8},{10,9},{11,1... | collective-permute-start | bytes 393224 | tf_op jit(solution)/shard_map/ppermute | solution.py:17
  357.6 498.1 %all-gather.14.cloned.1.call-start = ((), (), s32[]{:S(2)}) async-start(), calls=%async_computation.2 | async-start | bytes 25559040 | tf_op jit(solution)/shard_map/all_gather | solution.py:62
  636.2 15.9 %collective-permute-start.12 = (f32[1,256,128]{1,2,0:T(8,128)S(1)}, f32[1,256,128]{1,2,0:T(8,128)S(1)}, u32[]{:S(2)}, u32[]{:S(2)}) collective-permute-start(f32[1,256,128]{1,2,0:T(8,128)S(1)} %get-tuple-element.32), channel_id=1, source_target_pairs={{0,1},{1,2},{2,3},{3,4},{4,5},{5,6},{6,7},{7,8},{8,9},{9,10},{10,1... | collective-permute-start | bytes 393224 | tf_op jit(solution)/shard_map/ppermute | solution.py:16
  638.5 13.7 %collective-permute-start.13 = (f32[1,256,128]{1,2,0:T(8,128)S(1)}, f32[1,256,128]{1,2,0:T(8,128)S(1)}, u32[]{:S(2)}, u32[]{:S(2)}) collective-permute-start(f32[1,256,128]{1,2,0:T(8,128)S(1)} %get-tuple-element.35), channel_id=1, source_target_pairs={{1,0},{2,1},{3,2},{4,3},{5,4},{6,5},{7,6},{8,7},{9,8},{10,9},{11,1... | collective-permute-start | bytes 393224 | tf_op jit(solution)/shard_map/ppermute | solution.py:17
  646.0 6.9 collective-permute-start.14
  650.2 9.0 collective-permute-start.15
  661.1 15.7 %collective-permute-start.16 = (f32[1,256,128]{2,1,0:T(8,128)S(1)}, f32[1,256,128]{2,1,0:T(8,128)S(1)}, u32[]{:S(2)}, u32[]{:S(2)}) collective-permute-start(f32[1,256,128]{2,1,0:T(8,128)S(1)} %get-tuple-element.24), channel_id=1, source_target_pairs={{0,1},{1,2},{2,3},{3,4},{4,5},{5,6},{6,7},{7,8},{8,9},{9,10},{10,1... | collective-permute-start | bytes 393224 | tf_op jit(solution)/shard_map/ppermute | solution.py:16
  663.0 13.7 %collective-permute-start.17 = (f32[1,256,128]{2,1,0:T(8,128)S(1)}, f32[1,256,128]{2,1,0:T(8,128)S(1)}, u32[]{:S(2)}, u32[]{:S(2)}) collective-permute-start(f32[1,256,128]{2,1,0:T(8,128)S(1)} %get-tuple-element.27), channel_id=1, source_target_pairs={{1,0},{2,1},{3,2},{4,3},{5,4},{6,5},{7,6},{8,7},{9,8},{10,9},{11,1... | collective-permute-start | bytes 393224 | tf_op jit(solution)/shard_map/ppermute | solution.py:17
  670.9 6.9 collective-permute-start.18
  672.8 9.0 collective-permute-start.19
  952.3 20.0 %collective-permute-start.20 = (f32[1,256,128]{1,2,0:T(8,128)}, f32[1,256,128]{1,2,0:T(8,128)S(1)}, u32[]{:S(2)}, u32[]{:S(2)}) collective-permute-start(f32[1,256,128]{1,2,0:T(8,128)} %get-tuple-element.16), channel_id=1, source_target_pairs={{0,1},{1,2},{2,3},{3,4},{4,5},{5,6},{6,7},{7,8},{8,9},{9,10},{10,1... | collective-permute-start | bytes 393224 | tf_op jit(solution)/shard_map/ppermute | solution.py:16
  954.5 17.8 %collective-permute-start.21 = (f32[1,256,128]{1,2,0:T(8,128)}, f32[1,256,128]{1,2,0:T(8,128)S(1)}, u32[]{:S(2)}, u32[]{:S(2)}) collective-permute-start(f32[1,256,128]{1,2,0:T(8,128)} %get-tuple-element.19), channel_id=1, source_target_pairs={{1,0},{2,1},{3,2},{4,3},{5,4},{6,5},{7,6},{8,7},{9,8},{10,9},{11,1... | collective-permute-start | bytes 393224 | tf_op jit(solution)/shard_map/ppermute | solution.py:17
  962.0 10.2 %collective-permute-start.22 = (f32[1,256,128]{1,2,0:T(8,128)S(1)}, f32[1,256,128]{1,2,0:T(8,128)S(1)}, u32[]{:S(2)}, u32[]{:S(2)}) collective-permute-start(f32[1,256,128]{1,2,0:T(8,128)S(1)} %get-tuple-element.17), channel_id=1, source_target_pairs={{0,64},{64,128},{128,192},{192,256},{256,320},{320,384},{384,448},... | collective-permute-start | bytes 393224 | tf_op jit(solution)/shard_map/ppermute | solution.py:16
  966.2 9.1 collective-permute-start.23
  (2 other events, 2.2 us)
Sparse Core Ops, SparseCore 0:
  40.9 172.9 all-gather.9
  357.7 174.6 all-gather.11
  683.8 171.8 all-gather.13
